TPU v7x, 512 devices: a whole 4x4x16 slice. The times are simulated.
512 devices in a mesh: seq: 128 (over x, z, core), head: 4 (over y).
Axes of the slice: x: 4, y: 4, z: 16, core: 2. Of those that a mesh axis runs over, the one named last changes fastest.
Arguments:
- queries: bfloat16 [65536, 2048], P('seq', 'head'), may hold values from -6 to 6
- keys: bfloat16 [65536, 2048], P('seq', 'head'), may hold values from -6 to 6
- values: bfloat16 [65536, 2048], P('seq', 'head'), may hold values from -6 to 6
- summary_lists: int32 [128, 8, 16], P('seq', 'head'), may hold values from 0 to 126, as said below
- out_weight: bfloat16 [2048, 2048], P('head'), may hold values from -0.125 to 0.125
Outputs:
- mixed: bfloat16 [65536, 2048], P(('seq', 'head'))
Inputs may be any that keep to these rules, and one draw needn't show every extreme that they name: `summary_lists`: entry [b, f, k] names a block. In every query block b above 0 it is below b, and entry [b, f, 0] is b - 1; in query block 0 every entry is 0 and names nothing. Entries may repeat.
All inputs are finite; a program needn't handle non-finite values.
Results may differ from a plain program's by a relative error of at most 0.014.
Values may be sent and summed in bfloat16 or wider, within the bound.
A program may use at most 64 MiB of HBM per device.

v0:
```python
import math

import jax
import jax.numpy as jnp
from jax import lax
from jax.sharding import PartitionSpec as P

HEAD_DIM = 128
BLK = 512
SUMMARY = 32
ROWS_DEV = 1


NEG = -1e30


def softmax_rounded(scores, valid):
    scores = jnp.where(valid, scores, NEG)
    peak = jnp.max(scores, axis=-1, keepdims=True)
    weights = jnp.where(valid, jnp.exp(scores - peak), 0.0)
    return (weights / jnp.sum(weights, axis=-1, keepdims=True)).astype(jnp.bfloat16)


def column_attend(pieces):
    col_q, col_k, col_v = pieces
    scale = HEAD_DIM ** (-0.5)
    scores = jnp.einsum("rxcd,sxcd->xcrs", col_q, col_k, preferred_element_type=jnp.float32) * scale
    blocks = col_q.shape[0]
    earlier = jnp.arange(blocks)[:, None] >= jnp.arange(blocks)[None, :]
    weights = softmax_rounded(scores, earlier)
    return jnp.einsum("xcrs,sxcd->rxcd", weights, col_v, preferred_element_type=jnp.float32).astype(
        jnp.bfloat16
    )


def absorb(state, scores, multiplier):
    old_peak, old_denom = (state[0], state[1])
    new_peak = jnp.maximum(old_peak, jnp.max(scores, axis=(3, 4)))
    weights = jnp.exp(scores - new_peak[..., None, None]) * multiplier[:, :, None, :, None]
    shrink = jnp.exp(old_peak - new_peak)
    return (new_peak, old_denom * shrink + jnp.sum(weights, axis=(3, 4)), shrink, weights)


def per_device(queries, keys, values, summary_lists, out_weight):
    scale = HEAD_DIM ** (-0.5)
    seq_count = lax.axis_size("seq")
    query_heads = queries.reshape(ROWS_DEV, BLK, 4, HEAD_DIM)
    key_heads = keys.reshape(ROWS_DEV, BLK, 4, HEAD_DIM)
    value_heads = values.reshape(ROWS_DEV, BLK, 4, HEAD_DIM)
    causal = jnp.arange(BLK)[:, None] >= jnp.arange(BLK)[None, :]
    block_index = lax.axis_index("seq") * ROWS_DEV + jnp.arange(ROWS_DEV, dtype=jnp.int32)

    def column_layout(source):
        return source[:, :, 1].reshape(ROWS_DEV, seq_count, BLK // seq_count, HEAD_DIM)

    column_moved = column_attend(
        (
            lax.all_to_all(
                column_layout(query_heads), "seq", split_axis=1, concat_axis=0, tiled=True
            ),
            lax.all_to_all(
                column_layout(key_heads), "seq", split_axis=1, concat_axis=0, tiled=True
            ),
            lax.all_to_all(
                column_layout(value_heads), "seq", split_axis=1, concat_axis=0, tiled=True
            ),
        )
    )
    row_scores = (
        jnp.einsum(
            "rid,rjd->rij",
            query_heads[:, :, 0],
            key_heads[:, :, 0],
            preferred_element_type=jnp.float32,
        )
        * scale
    )
    row_weights = softmax_rounded(row_scores, causal)
    row_out = jnp.einsum(
        "rij,rjd->rid", row_weights, value_heads[:, :, 0], preferred_element_type=jnp.float32
    ).astype(jnp.bfloat16)
    fixed_q = query_heads[:, :, 2:]
    fixed_k = key_heads[:, :, 2:]
    fixed_v = value_heads[:, :, 2:]
    own_scores = (
        jnp.einsum("rifd,rjfd->rfij", fixed_q, fixed_k, preferred_element_type=jnp.float32) * scale
    )
    own_scores = jnp.where(causal, own_scores, NEG)
    own_peak = jnp.max(own_scores, axis=-1)
    own_weights = jnp.exp(own_scores - own_peak[..., None])
    own_denom = jnp.sum(own_weights, axis=-1)
    own_sum = jnp.einsum(
        "rfij,rjfd->rfid",
        own_weights.astype(jnp.bfloat16),
        fixed_v,
        preferred_element_type=jnp.float32,
    )
    tail_k = jnp.swapaxes(fixed_k[:, BLK - SUMMARY :], 1, 2)
    tail_v = jnp.swapaxes(fixed_v[:, BLK - SUMMARY :], 1, 2)
    piece_k = lax.all_gather(tail_k, "seq", axis=0, tiled=True)
    piece_v = lax.all_gather(tail_v, "seq", axis=0, tiled=True)
    arrived = piece_k.shape[0]
    stride = math.gcd(arrived, 8)

    def inner(turn, running):
        offset = turn * stride
        part_k = lax.dynamic_slice_in_dim(piece_k, offset, stride, 0)
        part_v = lax.dynamic_slice_in_dim(piece_v, offset, stride, 0)
        tile_index = offset + jnp.arange(stride, dtype=jnp.int32)
        matches = (summary_lists[:, :, :, None] == tile_index) & (
            tile_index < block_index[:, None, None, None]
        )
        multiplier = jnp.sum(matches.astype(jnp.float32), axis=2)
        scores = (
            jnp.einsum("rifd,nfcd->rfinc", fixed_q, part_k, preferred_element_type=jnp.float32)
            * scale
        )
        scores = jnp.where(multiplier[:, :, None, :, None] > 0, scores, NEG)
        new_peak, new_denom, shrink, weights = absorb(running, scores, multiplier)
        new_sum = running[2] * shrink[..., None] + jnp.einsum(
            "rfinc,nfcd->rfid",
            weights.astype(jnp.bfloat16),
            part_v,
            preferred_element_type=jnp.float32,
        )
        return (new_peak, new_denom, new_sum)

    final_peak, final_denom, final_sum = lax.fori_loop(
        0, arrived // stride, inner, (own_peak, own_denom, own_sum)
    )
    fixed_out = jnp.swapaxes((final_sum / final_denom[..., None]).astype(jnp.bfloat16), 1, 2)
    column_out = lax.all_to_all(
        column_moved, "seq", split_axis=0, concat_axis=1, tiled=True
    ).reshape(ROWS_DEV, BLK, HEAD_DIM)
    attended = jnp.concatenate(
        [row_out[:, :, None], column_out[:, :, None], fixed_out], axis=2
    ).reshape(ROWS_DEV * BLK, 4 * HEAD_DIM)
    return lax.psum_scatter(
        jnp.dot(attended, out_weight, preferred_element_type=jnp.float32).astype(jnp.bfloat16),
        "head",
        scatter_dimension=0,
        tiled=True,
    )


def solution(mesh):
    return jax.shard_map(
        per_device,
        mesh=mesh,
        in_specs=(
            P("seq", "head"),
            P("seq", "head"),
            P("seq", "head"),
            P("seq", "head", None),
            P("head", None),
        ),
        out_specs=P(("seq", "head"), None),
        check_vma=False,
    )
```

profile of v0, /device:TPU:1, one launch (start us, length us, event | category | flops | bytes accessed | tf_op | source)
XLA Modules:
  0.0 376.9 jit_solution(72792832093655614)
XLA Ops:
  6.5 1.4 copy.55
  8.1 0.8 copy.72
  8.9 1.3 copy.56
  10.2 0.7 copy.73
  11.0 1.3 copy.54
  12.2 0.7 copy.57
  13.0 20.4 %all-to-all-start = ((bf16[1,128,4,128]{3,2,0,1:T(4,128)(2,1)}), bf16[1,128,4,128]{3,2,0,1:T(4,128)(2,1)S(1)}, u32[]{:S(2)}, u32[]{:S(2)}) async-start(bf16[1,128,4,128]{3,2,0,1:T(4,128)(2,1)} %bitcast.23), calls=%async_computation | async-start | bytes 262144 | tf_op jit(solution)/shard_map/all_to_all | solution.py:58
  33.4 0.7 copy.60
  34.1 1.3 fusion.47
  35.5 15.8 %all-to-all-done = bf16[1,128,4,128]{3,2,0,1:T(4,128)(2,1)S(1)} async-done(((bf16[1,128,4,128]{3,2,0,1:T(4,128)(2,1)}), bf16[1,128,4,128]{3,2,0,1:T(4,128)(2,1)S(1)}, u32[]{:S(2)}, u32[]{:S(2)}) %all-to-all-start) | async-done | bytes 131104 | tf_op jit(solution)/shard_map/all_to_all | solution.py:58
  51.3 6.7 %all-to-all-start.1 = ((bf16[1,128,4,128]{3,2,0,1:T(4,128)(2,1)}), bf16[1,128,4,128]{3,2,0,1:T(4,128)(2,1)S(1)}, u32[]{:S(2)}, u32[]{:S(2)}) async-start(bf16[1,128,4,128]{3,2,0,1:T(4,128)(2,1)} %bitcast.26), calls=%async_computation.1 | async-start | bytes 262144 | tf_op jit(solution)/shard_map/all_to_all | solution.py:61
  58.1 0.9 slice.51
  59.0 0.8 copy.63
  59.8 1.4 fusion.30
  61.1 2.9 fusion.15
  64.0 11.7 %all-to-all-done.1 = bf16[1,128,4,128]{3,2,0,1:T(4,128)(2,1)S(1)} async-done(((bf16[1,128,4,128]{3,2,0,1:T(4,128)(2,1)}), bf16[1,128,4,128]{3,2,0,1:T(4,128)(2,1)S(1)}, u32[]{:S(2)}, u32[]{:S(2)}) %all-to-all-start.1) | async-done | bytes 131104 | tf_op jit(solution)/shard_map/all_to_all | solution.py:61
  75.7 6.7 %all-to-all-start.2 = ((bf16[1,128,4,128]{3,2,0,1:T(4,128)(2,1)}), bf16[1,128,4,128]{3,2,0,1:T(4,128)(2,1)S(1)}, u32[]{:S(2)}, u32[]{:S(2)}) async-start(bf16[1,128,4,128]{3,2,0,1:T(4,128)(2,1)} %bitcast.29), calls=%async_computation.2 | async-start | bytes 262144 | tf_op jit(solution)/shard_map/all_to_all | solution.py:64
  82.5 0.6 iota_compare_fusion.1
  83.3 2.3 fusion.23
  85.8 14.3 %all-to-all-done.2 = bf16[1,128,4,128]{3,2,0,1:T(4,128)(2,1)S(1)} async-done(((bf16[1,128,4,128]{3,2,0,1:T(4,128)(2,1)}), bf16[1,128,4,128]{3,2,0,1:T(4,128)(2,1)S(1)}, u32[]{:S(2)}, u32[]{:S(2)}) %all-to-all-start.2) | async-done | bytes 131104 | tf_op jit(solution)/shard_map/all_to_all | solution.py:64
  100.4 0.8 copy.67
  101.1 6.8 %all-to-all-start.3 = ((bf16[128,1,4,128]{3,2,1,0:T(4,128)(2,1)}), bf16[128,1,4,128]{3,2,1,0:T(4,128)(2,1)S(1)}, u32[]{:S(2)}, u32[]{:S(2)}) async-start(bf16[128,1,4,128]{3,2,1,0:T(4,128)(2,1)} %copy.67), calls=%async_computation.3 | async-start | bytes 262144 | tf_op jit(solution)/shard_map/all_to_all | solution.py:132
  108.2 2.2 fusion.17
  110.4 1.7 convolution_bitcast_fusion.1
  112.1 13.7 %all-to-all-done.3 = bf16[128,1,4,128]{3,2,1,0:T(4,128)(2,1)S(1)} async-done(((bf16[128,1,4,128]{3,2,1,0:T(4,128)(2,1)}), bf16[128,1,4,128]{3,2,1,0:T(4,128)(2,1)S(1)}, u32[]{:S(2)}, u32[]{:S(2)}) %all-to-all-start.3) | async-done | bytes 131104 | tf_op jit(solution)/shard_map/all_to_all | solution.py:132
  125.9 32.0 %all-gather.3.cloned.1.call-done = bf16[128,2,32,128]{3,2,1,0:T(8,128)(2,1)} async-done(((bf16[1,2,32,128]{3,2,1,0:T(8,128)(2,1)}), bf16[128,2,32,128]{3,2,1,0:T(8,128)(2,1)}) %all-gather.3.cloned.1.call-update) | async-done | bytes 2097168 | tf_op jit(solution)/shard_map/all_gather | solution.py:100
  157.9 140.1 %all-gather.5.cloned.1.call-done = bf16[128,2,32,128]{3,2,1,0:T(8,128)(2,1)} async-done(((bf16[1,2,32,128]{3,2,1,0:T(8,128)(2,1)}), bf16[128,2,32,128]{3,2,1,0:T(8,128)(2,1)}) %all-gather.5.cloned.1.call-update) | async-done | bytes 2097168 | tf_op jit(solution)/shard_map/all_gather | solution.py:101
  298.1 36.2 %while.17 = (s32[]{:T(128)}, f32[1,2,512]{2,1,0:T(2,128)S(1)}, f32[1,2,512]{2,1,0:T(2,128)S(1)}, f32[1,2,512,128]{2,3,1,0:T(8,128)S(1)}, s32[1,2,16]{2,1,0:T(2,1...) while((s32[]{:T(128)}, f32[1,2,512]{2,1,0:T(2,128)S(1)}, ...), condition=%wide.region_10.11_spmd, body=%wide.region_6.10_spmd.sunk | while | flops 136843296 | bytes 5309099 | solution.py:128
  298.1 1.0 constant_dynamic-slice_fusion.3
  299.6 0.4 fusion.65
  300.3 1.0 constant_dynamic-slice_fusion.3
  301.9 0.4 fusion.65
  302.6 1.0 constant_dynamic-slice_fusion.3
  304.1 0.4 fusion.65
  304.9 1.0 constant_dynamic-slice_fusion.3
  306.4 0.4 fusion.65
  307.1 1.0 constant_dynamic-slice_fusion.3
  308.3 0.3 fusion.62
  308.6 0.4 fusion.65
  309.4 1.0 constant_dynamic-slice_fusion.3
  310.9 0.4 fusion.65
  311.6 1.0 constant_dynamic-slice_fusion.3
  313.2 0.4 fusion.65
  313.9 1.0 constant_dynamic-slice_fusion.3
  315.4 0.4 fusion.65
  316.2 1.0 constant_dynamic-slice_fusion.3
  317.3 0.3 fusion.62
  317.7 0.4 fusion.65
  318.4 1.0 constant_dynamic-slice_fusion.3
  319.9 0.4 fusion.65
  320.7 1.0 constant_dynamic-slice_fusion.3
  322.2 0.4 fusion.65
  322.9 1.0 constant_dynamic-slice_fusion.3
  324.5 0.4 fusion.65
  325.2 1.0 constant_dynamic-slice_fusion.3
  326.7 0.4 fusion.65
  327.4 1.0 constant_dynamic-slice_fusion.3
  329.0 0.4 fusion.65
  329.7 1.0 constant_dynamic-slice_fusion.3
  331.2 0.4 fusion.65
  332.0 1.0 constant_dynamic-slice_fusion.3
  333.5 0.4 fusion.65
  334.4 2.6 convolution_convert_fusion
  337.0 33.4 %reduce-scatter.2.cloned.1.call-done = bf16[128,2048]{1,0:T(8,128)(2,1)} async-done(((bf16[512,2048]{1,0:T(8,128)(2,1)}), bf16[128,2048]{1,0:T(8,128)(2,1)}) %reduce-scatter.2.cloned.1.call-update) | async-done | bytes 524304 | tf_op jit(solution)/shard_map/reduce_scatter | solution.py:138
  (174 shorter events, 13.3 us)
Async XLA Ops:
  6.5 327.8 %copy-start = (bf16[512,2048]{1,0:T(8,128)(2,1)S(1)}, bf16[512,2048]{1,0:T(8,128)(2,1)}, u32[]{:S(2)}) copy-start(bf16[512,2048]{1,0:T(8,128)(2,1)} %param.11) | copy-start | bytes 6291460
  6.5 151.4 %all-gather.3.cloned.1.call-start = ((), (), s32[]{:S(2)}) async-start(), calls=%async_computation.5 | async-start | bytes 2113536 | tf_op jit(solution)/shard_map/all_gather | solution.py:100
  7.9 27.5 %copy-start.3 = (bf16[512,512]{0,1:T(8,128)(2,1)}, bf16[512,512]{0,1:T(8,128)(2,1)S(1)}, u32[]{:S(2)}) copy-start(bf16[512,512]{0,1:T(8,128)(2,1)S(1)} %copy.55) | copy-start | bytes 1572868
  8.8 289.2 %all-gather.5.cloned.1.call-start = ((), (), s32[]{:S(2)}) async-start(), calls=%async_computation.6 | async-start | bytes 2113536 | tf_op jit(solution)/shard_map/all_gather | solution.py:101
  10.1 0.8 copy-start.2
  13.0 38.3 %all-to-all-start = ((bf16[1,128,4,128]{3,2,0,1:T(4,128)(2,1)}), bf16[1,128,4,128]{3,2,0,1:T(4,128)(2,1)S(1)}, u32[]{:S(2)}, u32[]{:S(2)}) async-start(bf16[1,128,4,128]{3,2,0,1:T(4,128)(2,1)} %bitcast.23), calls=%async_computation | async-start | bytes 262144 | tf_op jit(solution)/shard_map/all_to_all | solution.py:58
  51.3 24.4 %all-to-all-start.1 = ((bf16[1,128,4,128]{3,2,0,1:T(4,128)(2,1)}), bf16[1,128,4,128]{3,2,0,1:T(4,128)(2,1)S(1)}, u32[]{:S(2)}, u32[]{:S(2)}) async-start(bf16[1,128,4,128]{3,2,0,1:T(4,128)(2,1)} %bitcast.26), calls=%async_computation.1 | async-start | bytes 262144 | tf_op jit(solution)/shard_map/all_to_all | solution.py:61
  75.7 24.4 %all-to-all-start.2 = ((bf16[1,128,4,128]{3,2,0,1:T(4,128)(2,1)}), bf16[1,128,4,128]{3,2,0,1:T(4,128)(2,1)S(1)}, u32[]{:S(2)}, u32[]{:S(2)}) async-start(bf16[1,128,4,128]{3,2,0,1:T(4,128)(2,1)} %bitcast.29), calls=%async_computation.2 | async-start | bytes 262144 | tf_op jit(solution)/shard_map/all_to_all | solution.py:64
  83.3 2.3 copy-start.6
  101.1 24.7 %all-to-all-start.3 = ((bf16[128,1,4,128]{3,2,1,0:T(4,128)(2,1)}), bf16[128,1,4,128]{3,2,1,0:T(4,128)(2,1)S(1)}, u32[]{:S(2)}, u32[]{:S(2)}) async-start(bf16[128,1,4,128]{3,2,1,0:T(4,128)(2,1)} %copy.67), calls=%async_computation.3 | async-start | bytes 262144 | tf_op jit(solution)/shard_map/all_to_all | solution.py:132
  107.9 262.5 %reduce-scatter.2.cloned.1.call-start = ((), (), s32[]{:S(2)}) async-start(), calls=%async_computation.7 | async-start | bytes 2621440 | tf_op jit(solution)/shard_map/reduce_scatter | solution.py:138
  108.2 2.2 copy-start.1
  110.4 187.6 %copy-start.5 = (s32[1,2,16]{2,1,0:T(2,128)S(1)}, s32[1,2,16]{2,1,0:T(2,128)}, u32[]{:S(2)}) copy-start(s32[1,2,16]{2,1,0:T(2,128)} %param.10) | copy-start | bytes 388
  298.1 36.2 %copy-start.4 = (bf16[1,512,1,128]{1,3,2,0:T(8,128)(2,1)S(1)}, bf16[1,512,1,128]{1,3,2,0:T(8,128)(2,1)}, u32[]{:S(2)}) copy-start(bf16[1,512,1,128]{1,3,2,0:T(8,128)(2,1)} %fusion.23) | copy-start | bytes 393220
Sparse Core Ops, SparseCore 0:
  10.5 147.4 all-gather.2
  161.1 136.9 all-gather.4
  337.1 33.2 reduce-scatter.1
where the time goes:
time: 378 us; the launch traced here: 377 us
  waiting for transfers between devices  261 us (69%)
  starting transfers between devices  40.9 us (11%)
  local copies, waits for them, and re-layouts  25.7 us (7%)
  matrix products  23.2 us (6%)
  between operations  13.3 us (4%)
  other arithmetic  11.7 us (3%)
    all_gather x1, waiting for transfers between devices, per_device(): piece_v = lax.all_gather(tail_v, 'seq', axis=0, tiled=True)  140 us
    reduce_scatter x1, waiting for transfers between devices, per_device(): lax.psum_scatter(jnp.dot(attended, out_weight, preferred_element_type=jnp...  33.4 us
    all_gather x1, waiting for transfers between devices, per_device(): piece_k = lax.all_gather(tail_k, 'seq', axis=0, tiled=True)  32 us
    all_to_all x1, starting transfers between devices, per_device(): lax.all_to_all(column_layout(query_heads), 'seq', split_axis=1, concat_ax...  20.4 us
    dynamic_slice x16, local copies, waits for them, and re-layouts, inner(): part_v = lax.dynamic_slice_in_dim(piece_v, offset, stride, 0)  15.9 us
    all_to_all x1, waiting for transfers between devices, per_device(): lax.all_to_all(column_layout(query_heads), 'seq', split_axis=1, concat_ax...  15.8 us
    all_to_all x1, waiting for transfers between devices, per_device(): lax.all_to_all(column_layout(value_heads), 'seq', split_axis=1, concat_ax...  14.3 us
    all_to_all x1, waiting for transfers between devices, per_device(): lax.all_to_all(column_moved, 'seq', split_axis=0, concat_axis=1, tiled=True)  13.7 us
  transfers between devices with their start and end apart: 7, of which 7 were waited for; matrix products, arithmetic and copies ran while one was open for 5% of the time, Pallas kernels for 0%

commit v1 on v0

v1 whole, which is shorter than its diff:
```python
import functools
import math

import jax
import jax.numpy as jnp
from jax import lax
from jax.experimental import pallas as pl
from jax.experimental.pallas import tpu as pltpu
from jax.sharding import PartitionSpec as P

MESH = pl.DeviceIdType.MESH
HD = 128
BLK = 512
NX, NZ, NC, NY = 4, 16, 2, 4
PICKS = 16
SUM = 32
NEG = -1e30
EXPC = (HD ** -0.5) * math.log2(math.e)
QC = 256
OC = 0
BF = jnp.bfloat16
F32 = jnp.float32


def dot_t(a, b):
    return lax.dot_general(a, b, (((1,), (1,)), ((), ())), preferred_element_type=F32)


def dot(a, b):
    return jnp.dot(a, b, preferred_element_type=F32)


def kernel(
    lists, q, k, v, q3, k3, v3, k2, v2, w,
    out,
    tiles, wbuf, abuf, stage, c1, c2, obuf, r1, colout, orow, ofix,
    cf, cfo, acc_s, m_s, l_s, fark, farv, pbuf, prcv,
    lsem, wlsem, wssem, wrsem, tsend, zl, zr, xl, xr, x2sem, psem,
    a2s, a2r, p2s, p2r, r1s, r1r, r2s, r2r, ysend, asem, fsend, frecv,
):
    seq = lax.axis_index("seq")
    y = lax.axis_index("head")
    x = seq // (NZ * NC)
    z = (seq // NC) % NZ
    c = seq % NC
    oth = 1 - c

    def dev(xx, zz, cc, yy):
        return ((xx * NZ + zz) * NC + cc, yy)

    def rcopy(src, dst, ss, rs, to):
        return pltpu.make_async_remote_copy(
            src_ref=src, dst_ref=dst, send_sem=ss, recv_sem=rs, device_id=to, device_id_type=MESH
        )

    def wait_bytes(ref, sem):
        pltpu.make_async_copy(ref, ref, sem).wait()

    bar = pltpu.get_barrier_semaphore()

    def greet(to):
        pl.semaphore_signal(bar, inc=1, device_id=to, device_id_type=MESH)

    def greet_z(i, carry):
        greet(dev(x, (z + i) % NZ, c, y))
        return carry

    lax.fori_loop(1, NZ, greet_z, 0)
    for dx in range(NX):
        for dc in range(NC):
            if dx or dc:
                greet(dev((x + dx) % NX, z, (c + dc) % NC, y))
    for dy in range(1, NY):
        for dc in range(NC):
            greet(dev(x, z, (c + dc) % NC, (y + dy) % NY))

    own = c * 64 + x * NZ + z
    local = []
    for t, src in enumerate((q3, k3, v3)):
        local.append(pltpu.make_async_copy(src.at[:, :, HD : 2 * HD], stage.at[t], lsem.at[t]))
    for f in range(2):
        for t, src in enumerate((k2, v2)):
            local.append(
                pltpu.make_async_copy(
                    src.at[BLK - SUM : BLK, (2 + f) * HD : (3 + f) * HD],
                    tiles.at[own, f, t],
                    lsem.at[3 + 2 * f + t],
                )
            )
    for h in range(2):
        local.append(
            pltpu.make_async_copy(
                w.at[pl.ds(pl.multiple_of((2 * h + c) * HD, HD), HD)],
                wbuf.at[pl.ds(pl.multiple_of((y * 2 + h) * HD, HD), HD)],
                wlsem.at[h],
            )
        )
    for cp in local:
        cp.start()

    def own_attention(head, i):
        qi = q[i * QC : (i + 1) * QC, head * HD : (head + 1) * HD]
        n = (i + 1) * QC
        s = dot_t(qi, k[:n, head * HD : (head + 1) * HD])
        rows = lax.broadcasted_iota(jnp.int32, (QC, n), 0) + i * QC
        cols = lax.broadcasted_iota(jnp.int32, (QC, n), 1)
        s = jnp.where(rows >= cols, s, NEG)
        m = jnp.max(s, axis=1, keepdims=True)
        p = jnp.exp2((s - m) * EXPC)
        l = jnp.sum(p, axis=1, keepdims=True)
        acc = dot(p.astype(BF), v[:n, head * HD : (head + 1) * HD])
        return m, l, acc

    for i in range(BLK // QC):
        m, l, acc = own_attention(0, i)
        orow[i * (QC // 8) : (i + 1) * (QC // 8)] = (acc / l).astype(BF).reshape(QC // 8, 8, HD)
    for f in range(2):
        for i in range(BLK // QC):
            m, l, acc = own_attention(2 + f, i)
            rs = slice(i * QC, (i + 1) * QC)
            acc_s[f, rs, :] = acc
            m_s[f, rs, :] = jnp.broadcast_to(m, (QC, HD))
            l_s[f, rs, :] = jnp.broadcast_to(l, (QC, HD))

    for cp in local:
        cp.wait()
    pl.semaphore_wait(bar, (NZ - 1) + (NX * NC - 1) + (NY - 1) * NC)

    def wrows(yy, h):
        return wbuf.at[pl.ds(pl.multiple_of((yy * 2 + h) * HD, HD), HD)]

    yr, yl, y2 = (y + 1) % NY, (y + NY - 1) % NY, (y + 2) % NY
    wsends = []

    def wsend(n, yy, h, to, rsem):
        cp = rcopy(wrows(yy, h), wrows(yy, h), wssem.at[n], rsem, dev(x, z, c, to))
        cp.start()
        wsends.append(cp)

    def wsend_first():
        wsend(0, y, 0, yr, wrsem.at[0])
        wsend(1, y, 1, yl, wrsem.at[3])
        wsend(2, y, 1, yr, wrsem.at[1])
        wsend(3, y, 0, yl, wrsem.at[2])

    def wrelay():
        wait_bytes(wrows(yl, 0), wrsem.at[0])
        wsend(4, yl, 0, yr, wrsem.at[4])
        wait_bytes(wrows(yr, 1), wrsem.at[3])
        wsend(5, yr, 1, yl, wrsem.at[5])

    ysends = []

    def attended_send(n, src_of, tc, h):
        lanes = pl.ds(pl.multiple_of((y * 2 + h) * HD, HD), HD)
        dst = abuf.at[c, :, :, lanes]
        for dy in range(1, NY):
            yy = (y + dy) % NY
            cp = rcopy(src_of(yy), dst, ysend.at[n, dy], asem, dev(x, z, tc, yy))
            cp.start()
            ysends.append((cp, None))
        near = rcopy(src_of(y), dst, ysend.at[n, 0], asem, dev(x, z, oth, y))
        ysends.append((near, tc))

        @pl.when(c == tc)
        def _():
            pltpu.make_async_copy(src_of(y), dst, asem).start()

        @pl.when(c != tc)
        def _():
            near.start()

    def quarter(ref):
        return lambda yy: ref.at[pl.ds(pl.multiple_of(yy * 16, 16), 16)]

    xr_, xl_, x2_ = (x + 1) % NX, (x + NX - 1) % NX, (x + 2) % NX

    def slot(xx, zz):
        return c * 64 + xx * NZ + zz

    def zm(d):
        return (z + d + NZ) % NZ

    def tsend_to(src, rs, to):
        rcopy(src, src, tsend, rs, to).start()

    def ring_send(s):
        right, left = dev(x, zm(1), c, y), dev(x, zm(-1), c, y)
        if s < 8:
            tsend_to(tiles.at[slot(x, zm(1 - s))], zl.at[s], right)
            tsend_to(tiles.at[slot(x, zm(s - 1))], zr.at[s], left)
        else:
            tsend_to(tiles.at[slot(x, zm(-7)), 0], zl.at[8], right)
            tsend_to(tiles.at[slot(x, zm(7)), 1], zr.at[8], left)

    def ring_wait(s):
        if s < 8:
            wait_bytes(tiles.at[slot(x, zm(-s))], zl.at[s])
            wait_bytes(tiles.at[slot(x, zm(s))], zr.at[s])
        else:
            wait_bytes(tiles.at[slot(x, zm(8)), 0], zl.at[8])
            wait_bytes(tiles.at[slot(x, zm(8)), 1], zr.at[8])

    def members(n):
        if n == 0:
            return [z]
        if n == 8:
            return [zm(8)]
        return [zm(-n), zm(n)]

    partner = dev(x, z, oth, y)

    def forward(n):
        for zz in members(n):
            src = tiles.at[slot(x, zz)]
            tsend_to(src, xl.at[zz], dev(xr_, z, c, y))
            tsend_to(src, xr.at[zz], dev(xl_, z, c, y))
            tsend_to(src, psem, partner)

    def relay(n):
        for zz in members(n):
            src = tiles.at[slot(xl_, zz)]
            wait_bytes(src, xl.at[zz])
            tsend_to(src.at[0], x2sem.at[0], dev(xr_, z, c, y))
            tsend_to(src, psem, partner)
            src = tiles.at[slot(xr_, zz)]
            wait_bytes(src, xr.at[zz])
            tsend_to(src.at[1], x2sem.at[1], dev(xl_, z, c, y))
            tsend_to(src, psem, partner)

    def col_send(d):
        zz = zm(d)
        rcopy(
            stage.at[:, pl.ds(zz * 4, 4)], c1.at[z], a2s, a2r.at[z], dev(x, zz, c, y)
        ).start()

    own_piece = pltpu.make_async_copy(stage.at[:, pl.ds(z * 4, 4)], c1.at[z], lsem.at[7])
    own_piece.start()

    wsend_first()
    for s in range(1, 9):
        ring_send(s)
        if s == 1:
            col_send(8)
        else:
            col_send(9 - s)
            col_send(s - 9)
        forward(s - 1)
        if s >= 2:
            relay(s - 2)
        if s == 2:
            attended_send(0, quarter(orow), 0, 0)
        if s == 6:
            wrelay()
        ring_wait(s)
    forward(8)

    own_piece.wait()
    for d in range(1, NZ):
        zz = zm(d)
        wait_bytes(c1.at[zz], a2r.at[zz])
    src_id = x * NC + c
    p2 = []
    for dx in range(NX):
        g = (x + dx) % NX
        p2.append(rcopy(c1.at[:, :, g], c2.at[src_id], p2s.at[dx], p2r, dev(g, z, OC, y)))
    for dx in range(1, NX):
        p2[dx].start()

    @pl.when(c == OC)
    def _():
        pltpu.make_async_copy(c1.at[:, :, x], c2.at[src_id], p2r).start()

    @pl.when(c != OC)
    def _():
        p2[0].start()

    relay(7)
    relay(8)
    far2 = tiles.at[pl.ds(slot(x2_, 0), NZ)]
    wait_bytes(far2.at[:, 0], x2sem.at[0])
    wait_bytes(far2.at[:, 1], x2sem.at[1])
    tsend_to(far2, psem, partner)

    @pl.when(c == OC)
    def _():
        wait_bytes(c2, p2r)
        for t in range(3):
            cf[t] = c2[:, :, t].astype(F32).reshape(NBLK8, HD)

        def blk(r):
            return (r // 32) * 32 + (r % 16) * 2 + (r // 16) % 2

        rq = blk(lax.broadcasted_iota(jnp.int32, (128, 128), 0))
        rk = blk(lax.broadcasted_iota(jnp.int32, (128, 128), 1))
        ok = rq >= rk
        for j in range(8):
            cols = pl.ds(j, 128, stride=8)
            qc = cf[0, cols, :].astype(BF)
            kc = cf[1, cols, :].astype(BF)
            vc = cf[2, cols, :].astype(BF)
            s = jnp.where(ok, dot_t(qc, kc), NEG)
            m = jnp.max(s, axis=1, keepdims=True)
            p = jnp.exp2((s - m) * EXPC)
            l = jnp.sum(p, axis=1, keepdims=True)
            cfo[cols, :] = dot(p.astype(BF), vc) / l
        obuf[...] = cfo[...].astype(BF).reshape(NX * NC, NZ, 8, HD)
        for dx in range(NX):
            for dc in range(NC):
                if dx or dc:
                    xx, cc = (x + dx) % NX, (c + dc) % NC
                    rcopy(obuf.at[xx * NC + cc], r1.at[x], r1s, r1r, dev(xx, z, cc, y)).start()
        pltpu.make_async_copy(obuf.at[x * NC + c], r1.at[x], r1r).start()

    wait_bytes(r1, r1r)
    for d in range(1, NZ):
        zz = zm(d)
        rcopy(
            r1.at[:, zz], colout.at[pl.ds(z * 4, 4)], r2s, r2r, dev(x, zz, c, y)
        ).start()
    pltpu.make_async_copy(r1.at[:, z], colout.at[pl.ds(z * 4, 4)], r2r).start()

    wait_bytes(tiles.at[pl.ds(oth * 64, 64)], psem)
    for f in range(2):
        for i in range(PICKS):
            t = lists[0, f, i]
            at = (t % 2) * 64 + t // 2
            fark[i * SUM : (i + 1) * SUM, :] = tiles[at, f, 0]
            farv[i * SUM : (i + 1) * SUM, :] = tiles[at, f, 1]
        for i in range(BLK // QC):
            rs = slice(i * QC, (i + 1) * QC)
            s = dot_t(q[rs, (2 + f) * HD : (3 + f) * HD], fark[...])
            s = jnp.where(jnp.full((QC, BLK), seq, jnp.int32) > 0, s, NEG)
            m0 = m_s[f, rs, :][:, :1]
            m = jnp.maximum(jnp.max(s, axis=1, keepdims=True), m0)
            p = jnp.exp2((s - m) * EXPC)
            shrink = jnp.exp2((m0 - m) * EXPC)
            l = l_s[f, rs, :][:, :1] * shrink + jnp.sum(p, axis=1, keepdims=True)
            acc = acc_s[f, rs, :] * shrink + dot(p.astype(BF), farv[...])
            ofix[f, i * (QC // 8) : (i + 1) * (QC // 8)] = (acc / l).astype(BF).reshape(QC // 8, 8, HD)
        attended_send(1 + f, quarter(ofix.at[f]), f, 1)

    wait_bytes(colout, r2r)
    attended_send(3, quarter(colout), 1, 0)

    wait_bytes(wrows(yl, 1), wrsem.at[1])
    wait_bytes(wrows(yr, 0), wrsem.at[2])
    wait_bytes(wrows(y2, 0), wrsem.at[4])
    wait_bytes(wrows(y2, 1), wrsem.at[5])
    wait_bytes(abuf, asem)
    psends = []
    ap = abuf[oth].reshape(128, 1024)
    for n in range(4):
        pbuf[n] = dot(ap, wbuf[:, n * 512 : (n + 1) * 512]).astype(BF)
        cp = rcopy(pbuf.at[n], prcv.at[n], fsend.at[n], frecv.at[n], partner)
        cp.start()
        psends.append(cp)
    ao = abuf[c].reshape(128, 1024)
    for n in range(4):
        po = dot(ao, wbuf[:, n * 512 : (n + 1) * 512])
        psends[n].wait_recv()
        out[:, n * 512 : (n + 1) * 512] = (po + prcv[n].astype(F32)).astype(BF)

    for cp in psends:
        cp.wait_send()
    for cp in wsends:
        cp.wait_send()
    for cp, tc in ysends:
        if tc is None:
            cp.wait_send()
        else:
            @pl.when(c != tc)
            def _():
                cp.wait_send()
    wait_bytes(tiles.at[pl.ds(0, 127)], tsend)
    wait_bytes(stage.at[:, pl.ds(0, 60)], a2s)
    for dx in range(1, NX):
        p2[dx].wait_send()

    @pl.when(c != OC)
    def _():
        p2[0].wait_send()

    @pl.when(c == OC)
    def _():
        wait_bytes(obuf.at[pl.ds(0, 7)], r1s)

    wait_bytes(r1.at[:, pl.ds(0, 15)], r2s)


NBLK8 = NX * NZ * NC * 8


def per_device(queries, keys, values, summary_lists, out_weight):
    q3, k3, v3 = (a.reshape(64, 8, 512) for a in (queries, keys, values))
    vm = pl.BlockSpec(memory_space=pltpu.VMEM)
    anys = pl.BlockSpec(memory_space=pl.ANY)
    dma = pltpu.SemaphoreType.DMA
    return pl.pallas_call(
        kernel,
        out_shape=jax.ShapeDtypeStruct((128, 2048), BF),
        in_specs=[pl.BlockSpec(memory_space=pltpu.SMEM)] + [vm] * 3 + [anys] * 6,
        out_specs=vm,
        scratch_shapes=[
            pltpu.VMEM((128, 2, 2, SUM, HD), BF),
            pltpu.VMEM((1024, 2048), BF),
            pltpu.VMEM((2, 16, 8, 1024), BF),
            pltpu.VMEM((3, 64, 8, HD), BF),
            pltpu.VMEM((NZ, 3, 4, 8, HD), BF),
            pltpu.VMEM((NX * NC, NZ, 3, 8, HD), BF),
            pltpu.VMEM((NX * NC, NZ, 8, HD), BF),
            pltpu.VMEM((NX, NZ, 8, HD), BF),
            pltpu.VMEM((64, 8, HD), BF),
            pltpu.VMEM((64, 8, HD), BF),
            pltpu.VMEM((2, 64, 8, HD), BF),
            pltpu.VMEM((3, NBLK8, HD), F32),
            pltpu.VMEM((NBLK8, HD), F32),
            pltpu.VMEM((2, BLK, HD), F32),
            pltpu.VMEM((2, BLK, HD), F32),
            pltpu.VMEM((2, BLK, HD), F32),
            pltpu.VMEM((BLK, HD), BF),
            pltpu.VMEM((BLK, HD), BF),
            pltpu.VMEM((4, 128, 512), BF),
            pltpu.VMEM((4, 128, 512), BF),
            dma((8,)), dma((2,)), dma((6,)), dma((6,)), dma, dma((9,)), dma((9,)), dma((16,)), dma((16,)), dma((2,)), dma,
            dma, dma((16,)), dma((4,)), dma, dma, dma, dma, dma, dma((4, 4)), dma, dma((4,)), dma((4,)),
        ],
        compiler_params=pltpu.CompilerParams(
            collective_id=0, has_side_effects=True, vmem_limit_bytes=48 * 1024 * 1024
        ),
    )(summary_lists, queries, keys, values, q3, k3, v3, keys, values, out_weight)


def solution(mesh):
    return jax.shard_map(
        per_device,
        mesh=mesh,
        in_specs=(
            P("seq", "head"),
            P("seq", "head"),
            P("seq", "head"),
            P("seq", "head", None),
            P("head", None),
        ),
        out_specs=P(("seq", "head"), None),
        check_vma=False,
    )
```

time: 378 us -> 88.6 us (0.23)
  waiting for transfers between devices: 261 us -> 0 us
  Pallas kernels: 0 us -> 82.1 us
  starting transfers between devices: 40.9 us -> 0 us
  matrix products: 23.2 us -> 0 us
  local copies, waits for them, and re-layouts: 25.7 us -> 6.19 us
  between operations: 13.3 us -> 0.01 us
  other arithmetic: 11.7 us -> 0 us
    all_gather x2 -> x0, waiting for transfers between devices: 172 us -> none  [the longest x1 140 us: per_device(): piece_v = lax.all_gather(tail_v, 'seq', axis=0, tiled=True)]
    pallas_call x0 -> x1, Pallas kernels: none -> 82.1 us  [per_device(): pl.pallas_call(kernel, out_shape=jax.ShapeDtypeStruct((128, 2048), BF), i...]
    all_to_all x4 -> x0, waiting for transfers between devices: 55.5 us -> none  [the longest x1 15.8 us: per_device(): lax.all_to_all(column_layout(query_heads), 'seq', split_axis=1, concat_ax...]
    all_to_all x4 -> x0, starting transfers between devices: 40.6 us -> none  [the longest x1 20.4 us: per_device(): lax.all_to_all(column_layout(query_heads), 'seq', split_axis=1, concat_ax...]
    reduce_scatter x1 -> x0, waiting for transfers between devices: 33.4 us -> none  [per_device(): lax.psum_scatter(jnp.dot(attended, out_weight, preferred_element_type=jnp...]
    dot_general x38 -> x0, matrix products: 22.9 us -> none  [the longest x16 6.79 us: inner(): jnp.einsum('rfinc,nfcd->rfid', weights.astype(jnp.bfloat16), part_v, pref...]
    dynamic_slice x16 -> x0, local copies, waits for them, and re-layouts: 15.9 us -> none  [inner(): part_v = lax.dynamic_slice_in_dim(piece_v, offset, stride, 0)]
    reduce_sum x34 -> x0, other arithmetic: 10.2 us -> none  [the longest x16 4.06 us: absorb(): jnp.sum(weights, axis=(3, 4))]
  transfers between devices with their start and end apart: 7 -> 0, of which waited for: 7 -> 0; matrix products, arithmetic and copies ran while one was open for 5% -> 0% of each run, Pallas kernels for 0% -> 0%
where the time goes in v1:
time: 88.6 us; the launch traced here: 88.3 us
  Pallas kernels  82.1 us (93%)
  local copies, waits for them, and re-layouts  6.19 us (7%)
    pallas_call x1, Pallas kernels, per_device(): pl.pallas_call(kernel, out_shape=jax.ShapeDtypeStruct((128, 2048), BF), i...  82.1 us
    unnamed x11, local copies, waits for them, and re-layouts  6.19 us

profile of v1, /device:TPU:1, one launch (start us, length us, event | category | flops | bytes accessed | tf_op | source)
XLA Modules:
  0.0 88.3 jit_solution(18010771055702553140)
XLA Ops:
  0.0 0.0 copy-start
  0.0 1.0 %copy-done = bf16[512,512]{1,0:T(8,128)(2,1)S(1)} copy-done((bf16[512,512]{1,0:T(8,128)(2,1)S(1)}, bf16[512,512]{1,0:T(8,128)(2,1)}, u32[]{:S(2)}) %copy-start) | copy-done | bytes 524312
  1.0 0.0 copy-start.1
  1.0 1.0 %copy-done.1 = bf16[512,512]{1,0:T(8,128)(2,1)S(1)} copy-done((bf16[512,512]{1,0:T(8,128)(2,1)S(1)}, bf16[512,512]{1,0:T(8,128)(2,1)}, u32[]{:S(2)}) %copy-start.1) | copy-done | bytes 524312
  2.1 0.0 copy-start.2
  2.1 1.0 %copy-done.2 = bf16[512,512]{1,0:T(8,128)(2,1)S(1)} copy-done((bf16[512,512]{1,0:T(8,128)(2,1)S(1)}, bf16[512,512]{1,0:T(8,128)(2,1)}, u32[]{:S(2)}) %copy-start.2) | copy-done | bytes 524312
  3.1 0.0 copy-start.3
  3.1 1.6 %copy-done.3 = bf16[512,2048]{1,0:T(8,128)(2,1)S(1)} copy-done((bf16[512,2048]{1,0:T(8,128)(2,1)S(1)}, bf16[512,2048]{1,0:T(8,128)(2,1)}, u32[]{:S(2)}) %copy-start.3) | copy-done | bytes 2097176
  4.7 0.0 copy-start.4
  4.7 0.7 copy-done.4
  5.4 82.1 %shard_map.55 = bf16[128,2048]{1,0:T(8,128)(2,1)S(1)} custom-call(s32[1,2,16]{2,1,0:T(2,128)S(1)} %copy-done.4, bf16[512,512]{1,0:T(8,128)(2,1)S(1)} %copy-done.2, bf16[512,512]{1,0:T(8,128)(2,1)S(1)} %copy-done, bf16[512,512]{1,0:T(8,128)(2,1)S(1)} %copy-done.1, bf16[64,8,512]{2,1,0:T(8,128)(2,1)S(1)} %bitcast.5, bf16[64,8,512]{2,1,0:T(8,128)(2,1)S(1)} %bitcast.3, ...), custom_call_target="tpu_custom_call" | custom-call | tf_op jit(solution)/shard_map/pallas_call | solution.py:399
  87.5 0.8 copy.7
Async XLA Ops:
  0.0 1.0 %copy-start = (bf16[512,512]{1,0:T(8,128)(2,1)S(1)}, bf16[512,512]{1,0:T(8,128)(2,1)}, u32[]{:S(2)}) copy-start(bf16[512,512]{1,0:T(8,128)(2,1)} %k2.1) | copy-start | bytes 1572868
  1.0 1.0 %copy-start.1 = (bf16[512,512]{1,0:T(8,128)(2,1)S(1)}, bf16[512,512]{1,0:T(8,128)(2,1)}, u32[]{:S(2)}) copy-start(bf16[512,512]{1,0:T(8,128)(2,1)} %v2.1) | copy-start | bytes 1572868
  2.1 1.0 %copy-start.2 = (bf16[512,512]{1,0:T(8,128)(2,1)S(1)}, bf16[512,512]{1,0:T(8,128)(2,1)}, u32[]{:S(2)}) copy-start(bf16[512,512]{1,0:T(8,128)(2,1)} %q.1) | copy-start | bytes 1572868
  3.1 1.6 %copy-start.3 = (bf16[512,2048]{1,0:T(8,128)(2,1)S(1)}, bf16[512,2048]{1,0:T(8,128)(2,1)}, u32[]{:S(2)}) copy-start(bf16[512,2048]{1,0:T(8,128)(2,1)} %w.1) | copy-start | bytes 6291460
  4.7 0.7 copy-start.4

commit v2 on v1

--- a/solution.py
+++ b/solution.py
@@ -18,6 +18,7 @@
 EXPC = (HD ** -0.5) * math.log2(math.e)
 QC = 256
 OC = 0
+SENDS = ((8, 7, -7), (6, -6), (5, -5), (4, -4), (3, -3), (2, -2, 1, -1, 0), (), ())
 BF = jnp.bfloat16
 F32 = jnp.float32
 
@@ -31,12 +32,13 @@
 
 
 def kernel(
-    lists, q, k, v, q3, k3, v3, k2, v2, w,
+    lists_h, q_h, k_h, v_h, q3, k3, v3, w,
     out,
-    tiles, wbuf, abuf, stage, c1, c2, obuf, r1, colout, orow, ofix,
+    lists, q, k, v,
+    tiles, wbuf, abuf, stage, c2, obuf, orow, ofix,
     cf, cfo, acc_s, m_s, l_s, fark, farv, pbuf, prcv,
-    lsem, wlsem, wssem, wrsem, tsend, zl, zr, xl, xr, x2sem, psem,
-    a2s, a2r, p2s, p2r, r1s, r1r, r2s, r2r, ysend, asem, fsend, frecv,
+    qsem, lsem, wlsem, wssem, wrsem, tsend, zl, zr, xl, xr, x2sem, psem,
+    rowsem, a2s, a2r, r1s, ysend, asem, fsend, frecv,
 ):
     seq = lax.axis_index("seq")
     y = lax.axis_index("head")
@@ -55,6 +57,11 @@
 
     def wait_bytes(ref, sem):
         pltpu.make_async_copy(ref, ref, sem).wait()
+
+    loads = []
+    for t, (src, dst) in enumerate(((q_h, q), (k_h, k), (v_h, v))):
+        loads.append(pltpu.make_async_copy(src, dst, qsem.at[t]))
+        loads[-1].start()
 
     bar = pltpu.get_barrier_semaphore()
 
@@ -78,8 +85,9 @@
     local = []
     for t, src in enumerate((q3, k3, v3)):
         local.append(pltpu.make_async_copy(src.at[:, :, HD : 2 * HD], stage.at[t], lsem.at[t]))
+    local.append(pltpu.make_async_copy(lists_h, lists, lsem.at[8]))
     for f in range(2):
-        for t, src in enumerate((k2, v2)):
+        for t, src in enumerate((k_h, v_h)):
             local.append(
                 pltpu.make_async_copy(
                     src.at[BLK - SUM : BLK, (2 + f) * HD : (3 + f) * HD],
@@ -111,6 +119,8 @@
         acc = dot(p.astype(BF), v[:n, head * HD : (head + 1) * HD])
         return m, l, acc
 
+    for cp in loads:
+        cp.wait()
     for i in range(BLK // QC):
         m, l, acc = own_attention(0, i)
         orow[i * (QC // 8) : (i + 1) * (QC // 8)] = (acc / l).astype(BF).reshape(QC // 8, 8, HD)
@@ -125,6 +135,12 @@
     for cp in local:
         cp.wait()
     pl.semaphore_wait(bar, (NZ - 1) + (NX * NC - 1) + (NY - 1) * NC)
+    for dx in range(NX):
+        for dc in range(NC):
+            if dx or dc:
+                pl.semaphore_signal(
+                    rowsem, inc=1, device_id=dev((x + dx) % NX, z, (c + dc) % NC, y), device_id_type=MESH
+                )
 
     def wrows(yy, h):
         return wbuf.at[pl.ds(pl.multiple_of((yy * 2 + h) * HD, HD), HD)]
@@ -228,23 +244,31 @@
             tsend_to(src.at[1], x2sem.at[1], dev(xl_, z, c, y))
             tsend_to(src, psem, partner)
 
+    src_id = x * NC + c
+
     def col_send(d):
         zz = zm(d)
-        rcopy(
-            stage.at[:, pl.ds(zz * 4, 4)], c1.at[z], a2s, a2r.at[z], dev(x, zz, c, y)
-        ).start()
-
-    own_piece = pltpu.make_async_copy(stage.at[:, pl.ds(z * 4, 4)], c1.at[z], lsem.at[7])
-    own_piece.start()
-
+        for dx in range(NX):
+            g = (x + dx) % NX
+            cp = rcopy(stage.at[:, zz * 4 + g], c2.at[src_id, z], a2s, a2r, dev(g, zz, OC, y))
+            if d or dx:
+                cp.start()
+            else:
+
+                @pl.when(c == OC)
+                def _():
+                    pltpu.make_async_copy(stage.at[:, zz * 4 + g], c2.at[src_id, z], a2r).start()
+
+                @pl.when(c != OC)
+                def _():
+                    cp.start()
+
+    pl.semaphore_wait(rowsem, NX * NC - 1)
     wsend_first()
     for s in range(1, 9):
         ring_send(s)
-        if s == 1:
-            col_send(8)
-        else:
-            col_send(9 - s)
-            col_send(s - 9)
+        for d in SENDS[s - 1]:
+            col_send(d)
         forward(s - 1)
         if s >= 2:
             relay(s - 2)
@@ -255,36 +279,11 @@
         ring_wait(s)
     forward(8)
 
-    own_piece.wait()
-    for d in range(1, NZ):
-        zz = zm(d)
-        wait_bytes(c1.at[zz], a2r.at[zz])
-    src_id = x * NC + c
-    p2 = []
-    for dx in range(NX):
-        g = (x + dx) % NX
-        p2.append(rcopy(c1.at[:, :, g], c2.at[src_id], p2s.at[dx], p2r, dev(g, z, OC, y)))
-    for dx in range(1, NX):
-        p2[dx].start()
+    relay(7)
 
     @pl.when(c == OC)
     def _():
-        pltpu.make_async_copy(c1.at[:, :, x], c2.at[src_id], p2r).start()
-
-    @pl.when(c != OC)
-    def _():
-        p2[0].start()
-
-    relay(7)
-    relay(8)
-    far2 = tiles.at[pl.ds(slot(x2_, 0), NZ)]
-    wait_bytes(far2.at[:, 0], x2sem.at[0])
-    wait_bytes(far2.at[:, 1], x2sem.at[1])
-    tsend_to(far2, psem, partner)
-
-    @pl.when(c == OC)
-    def _():
-        wait_bytes(c2, p2r)
+        wait_bytes(c2, a2r)
         for t in range(3):
             cf[t] = c2[:, :, t].astype(F32).reshape(NBLK8, HD)
 
@@ -304,21 +303,24 @@
             p = jnp.exp2((s - m) * EXPC)
             l = jnp.sum(p, axis=1, keepdims=True)
             cfo[cols, :] = dot(p.astype(BF), vc) / l
-        obuf[...] = cfo[...].astype(BF).reshape(NX * NC, NZ, 8, HD)
-        for dx in range(NX):
-            for dc in range(NC):
-                if dx or dc:
-                    xx, cc = (x + dx) % NX, (c + dc) % NC
-                    rcopy(obuf.at[xx * NC + cc], r1.at[x], r1s, r1r, dev(xx, z, cc, y)).start()
-        pltpu.make_async_copy(obuf.at[x * NC + c], r1.at[x], r1r).start()
-
-    wait_bytes(r1, r1r)
-    for d in range(1, NZ):
-        zz = zm(d)
-        rcopy(
-            r1.at[:, zz], colout.at[pl.ds(z * 4, 4)], r2s, r2r, dev(x, zz, c, y)
-        ).start()
-    pltpu.make_async_copy(r1.at[:, z], colout.at[pl.ds(z * 4, 4)], r2r).start()
+        obuf[...] = cfo[...].astype(BF).reshape(NX, NC, NZ, 8, HD)
+        lanes = pl.ds(pl.multiple_of(y * 2 * HD, HD), HD)
+
+        def give_back(i, carry):
+            for dx in range(NX):
+                xx, zz = (x + dx) % NX, (z + i) % NZ
+                rcopy(
+                    obuf.at[xx, :, zz], abuf.at[:, (z % 4) * 4 + x, :, lanes], r1s, asem, dev(xx, zz, 1, z // 4)
+                ).start()
+            return carry
+
+        lax.fori_loop(0, NZ, give_back, 0)
+
+    relay(8)
+    far2 = tiles.at[pl.ds(slot(x2_, 0), NZ)]
+    wait_bytes(far2.at[:, 0], x2sem.at[0])
+    wait_bytes(far2.at[:, 1], x2sem.at[1])
+    tsend_to(far2, psem, partner)
 
     wait_bytes(tiles.at[pl.ds(oth * 64, 64)], psem)
     for f in range(2):
@@ -340,8 +342,6 @@
             ofix[f, i * (QC // 8) : (i + 1) * (QC // 8)] = (acc / l).astype(BF).reshape(QC // 8, 8, HD)
         attended_send(1 + f, quarter(ofix.at[f]), f, 1)
 
-    wait_bytes(colout, r2r)
-    attended_send(3, quarter(colout), 1, 0)
 
     wait_bytes(wrows(yl, 1), wrsem.at[1])
     wait_bytes(wrows(yr, 0), wrsem.at[2])
@@ -373,19 +373,15 @@
             def _():
                 cp.wait_send()
     wait_bytes(tiles.at[pl.ds(0, 127)], tsend)
-    wait_bytes(stage.at[:, pl.ds(0, 60)], a2s)
-    for dx in range(1, NX):
-        p2[dx].wait_send()
 
     @pl.when(c != OC)
     def _():
-        p2[0].wait_send()
+        wait_bytes(stage, a2s)
 
     @pl.when(c == OC)
     def _():
-        wait_bytes(obuf.at[pl.ds(0, 7)], r1s)
-
-    wait_bytes(r1.at[:, pl.ds(0, 15)], r2s)
+        wait_bytes(stage.at[:, pl.ds(0, 63)], a2s)
+        wait_bytes(obuf, r1s)
 
 
 NBLK8 = NX * NZ * NC * 8
@@ -399,18 +395,19 @@
     return pl.pallas_call(
         kernel,
         out_shape=jax.ShapeDtypeStruct((128, 2048), BF),
-        in_specs=[pl.BlockSpec(memory_space=pltpu.SMEM)] + [vm] * 3 + [anys] * 6,
+        in_specs=[anys] * 8,
         out_specs=vm,
         scratch_shapes=[
+            pltpu.SMEM((1, 2, PICKS), jnp.int32),
+            pltpu.VMEM((BLK, 512), BF),
+            pltpu.VMEM((BLK, 512), BF),
+            pltpu.VMEM((BLK, 512), BF),
             pltpu.VMEM((128, 2, 2, SUM, HD), BF),
             pltpu.VMEM((1024, 2048), BF),
             pltpu.VMEM((2, 16, 8, 1024), BF),
             pltpu.VMEM((3, 64, 8, HD), BF),
-            pltpu.VMEM((NZ, 3, 4, 8, HD), BF),
             pltpu.VMEM((NX * NC, NZ, 3, 8, HD), BF),
-            pltpu.VMEM((NX * NC, NZ, 8, HD), BF),
-            pltpu.VMEM((NX, NZ, 8, HD), BF),
-            pltpu.VMEM((64, 8, HD), BF),
+            pltpu.VMEM((NX, NC, NZ, 8, HD), BF),
             pltpu.VMEM((64, 8, HD), BF),
             pltpu.VMEM((2, 64, 8, HD), BF),
             pltpu.VMEM((3, NBLK8, HD), F32),
@@ -422,13 +419,13 @@
             pltpu.VMEM((BLK, HD), BF),
             pltpu.VMEM((4, 128, 512), BF),
             pltpu.VMEM((4, 128, 512), BF),
-            dma((8,)), dma((2,)), dma((6,)), dma((6,)), dma, dma((9,)), dma((9,)), dma((16,)), dma((16,)), dma((2,)), dma,
-            dma, dma((16,)), dma((4,)), dma, dma, dma, dma, dma, dma((4, 4)), dma, dma((4,)), dma((4,)),
+            dma((3,)), dma((9,)), dma((2,)), dma((6,)), dma((6,)), dma, dma((9,)), dma((9,)), dma((16,)), dma((16,)), dma((2,)), dma,
+            pltpu.SemaphoreType.REGULAR, dma, dma, dma, dma((3, 4)), dma, dma((4,)), dma((4,)),
         ],
         compiler_params=pltpu.CompilerParams(
-            collective_id=0, has_side_effects=True, vmem_limit_bytes=48 * 1024 * 1024
+            collective_id=0, has_side_effects=True, vmem_limit_bytes=67043328
         ),
-    )(summary_lists, queries, keys, values, q3, k3, v3, keys, values, out_weight)
+    )(summary_lists, queries, keys, values, q3, k3, v3, out_weight)
 
 
 def solution(mesh):

time: 88.6 us -> 75.1 us (0.85)
  Pallas kernels: 82.1 us -> 73 us
  local copies, waits for them, and re-layouts: 6.19 us -> 1.88 us
    pallas_call x1, Pallas kernels: 82.1 us -> 73 us  [per_device(): pl.pallas_call(kernel, out_shape=jax.ShapeDtypeStruct((128, 2048), BF), i...]
    unnamed x11 -> x1, local copies, waits for them, and re-layouts: 6.19 us -> 1.88 us
where the time goes in v2:
time: 75.1 us; the launch traced here: 74.9 us
  Pallas kernels  73 us (97%)
  local copies, waits for them, and re-layouts  1.88 us (3%)
    pallas_call x1, Pallas kernels, per_device(): pl.pallas_call(kernel, out_shape=jax.ShapeDtypeStruct((128, 2048), BF), i...  73 us
    unnamed x1, local copies, waits for them, and re-layouts  1.88 us

profile of v2, /device:TPU:1, one launch (start us, length us, event | category | flops | bytes accessed | tf_op | source)
XLA Modules:
  0.0 74.9 jit_solution(9977406833059693669)
XLA Ops:
  0.0 73.0 %shard_map.55 = bf16[128,2048]{1,0:T(8,128)(2,1)} custom-call(s32[1,2,16]{2,1,0:T(2,128)} %lists_h.1, bf16[512,512]{1,0:T(8,128)(2,1)} %q_h.1, bf16[512,512]{1,0:T(8,128)(2,1)} %k_h.1, bf16[512,512]{1,0:T(8,128)(2,1)} %v_h.1, bf16[64,8,512]{2,1,0:T(8,128)(2,1)} %bitcast.3, bf16[64,8,512]{2,1,0:T(8,128)(2,1)} %bitcast.4, bf16[64,8,512]{2,1,0:T(8,128)(2,1)} %bitcast.5, ...), custom_call_target="tpu_custom_call" | custom-call | tf_op jit(solution)/shard_map/pallas_call | solution.py:395
  73.1 1.9 %copy.7 = bf16[128,2048]{1,0:T(8,128)(2,1)} copy(bf16[128,2048]{1,0:T(8,128)(2,1)} %shard_map.55) | data formatting | bytes 1048576

commit v3 on v2

--- a/solution.py
+++ b/solution.py
@@ -18,7 +18,14 @@
 EXPC = (HD ** -0.5) * math.log2(math.e)
 QC = 256
 OC = 0
-SENDS = ((8, 7, -7), (6, -6), (5, -5), (4, -4), (3, -3), (2, -2, 1, -1, 0), (), ())
+ZGROUPS = ((0,), (-5, 5, -1, 1), (-6, 6, -4, 4, -2, 2), (-7, 7, -3, 3), (8,))
+ZSENDS = (
+    ((0, 5, None), (0, -5, None), (0, 1, None), (0, -1, None)),
+    ((-5, 1, None), (5, -1, None), (-5, -1, None), (5, 1, None), (-1, 1, None), (1, -1, None)),
+    ((-6, 1, None), (6, -1, None), (-4, -1, None), (4, 1, None)),
+    ((-7, 1, 0), (7, -1, 1)),
+)
+SENDS = ((8, 0, 1, -1), (7, -7, 6, -6), (5, -5, 4, -4), (3, -3, 2, -2))
 BF = jnp.bfloat16
 F32 = jnp.float32
 
@@ -35,9 +42,9 @@
     lists_h, q_h, k_h, v_h, q3, k3, v3, w,
     out,
     lists, q, k, v,
-    tiles, wbuf, abuf, stage, c2, obuf, orow, ofix,
+    tiles, wbuf, abuf, part, stage, c2, obuf, orow, ofix,
     cf, cfo, acc_s, m_s, l_s, fark, farv, pbuf, prcv,
-    qsem, lsem, wlsem, wssem, wrsem, tsend, zl, zr, xl, xr, x2sem, psem,
+    qsem, lsem, wlsem, wssem, wrsem, tsend, zsem, xl, xr, x2sem, psem,
     rowsem, a2s, a2r, r1s, ysend, asem, fsend, frecv,
 ):
     seq = lax.axis_index("seq")
@@ -84,7 +91,7 @@
     own = c * 64 + x * NZ + z
     local = []
     for t, src in enumerate((q3, k3, v3)):
-        local.append(pltpu.make_async_copy(src.at[:, :, HD : 2 * HD], stage.at[t], lsem.at[t]))
+        local.append(pltpu.make_async_copy(src.at[:, :, HD : 2 * HD], stage.at[:, t], lsem.at[t]))
     local.append(pltpu.make_async_copy(lists_h, lists, lsem.at[8]))
     for f in range(2):
         for t, src in enumerate((k_h, v_h)):
@@ -98,8 +105,8 @@
     for h in range(2):
         local.append(
             pltpu.make_async_copy(
-                w.at[pl.ds(pl.multiple_of((2 * h + c) * HD, HD), HD)],
-                wbuf.at[pl.ds(pl.multiple_of((y * 2 + h) * HD, HD), HD)],
+                w.at[pl.ds(pl.multiple_of((2 - c if h else 3 * c) * HD, HD), HD)],
+                wbuf.at[pl.ds(pl.multiple_of((h * NY + y) * HD, HD), HD)],
                 wlsem.at[h],
             )
         )
@@ -143,7 +150,7 @@
                 )
 
     def wrows(yy, h):
-        return wbuf.at[pl.ds(pl.multiple_of((yy * 2 + h) * HD, HD), HD)]
+        return wbuf.at[pl.ds(pl.multiple_of((h * NY + yy) * HD, HD), HD)]
 
     yr, yl, y2 = (y + 1) % NY, (y + NY - 1) % NY, (y + 2) % NY
     wsends = []
@@ -168,19 +175,18 @@
     ysends = []
 
     def attended_send(n, src_of, tc, h):
-        lanes = pl.ds(pl.multiple_of((y * 2 + h) * HD, HD), HD)
-        dst = abuf.at[c, :, :, lanes]
+        dst = abuf.at[h, c, :, :, pl.ds(pl.multiple_of(y * HD, HD), HD)]
         for dy in range(1, NY):
             yy = (y + dy) % NY
-            cp = rcopy(src_of(yy), dst, ysend.at[n, dy], asem, dev(x, z, tc, yy))
+            cp = rcopy(src_of(yy), dst, ysend.at[n, dy], asem.at[h], dev(x, z, tc, yy))
             cp.start()
             ysends.append((cp, None))
-        near = rcopy(src_of(y), dst, ysend.at[n, 0], asem, dev(x, z, oth, y))
+        near = rcopy(src_of(y), dst, ysend.at[n, 0], asem.at[h], dev(x, z, oth, y))
         ysends.append((near, tc))
 
         @pl.when(c == tc)
         def _():
-            pltpu.make_async_copy(src_of(y), dst, asem).start()
+            pltpu.make_async_copy(src_of(y), dst, asem.at[h]).start()
 
         @pl.when(c != tc)
         def _():
@@ -200,29 +206,24 @@
     def tsend_to(src, rs, to):
         rcopy(src, src, tsend, rs, to).start()
 
-    def ring_send(s):
-        right, left = dev(x, zm(1), c, y), dev(x, zm(-1), c, y)
-        if s < 8:
-            tsend_to(tiles.at[slot(x, zm(1 - s))], zl.at[s], right)
-            tsend_to(tiles.at[slot(x, zm(s - 1))], zr.at[s], left)
-        else:
-            tsend_to(tiles.at[slot(x, zm(-7)), 0], zl.at[8], right)
-            tsend_to(tiles.at[slot(x, zm(7)), 1], zr.at[8], left)
-
-    def ring_wait(s):
-        if s < 8:
-            wait_bytes(tiles.at[slot(x, zm(-s))], zl.at[s])
-            wait_bytes(tiles.at[slot(x, zm(s))], zr.at[s])
-        else:
-            wait_bytes(tiles.at[slot(x, zm(8)), 0], zl.at[8])
-            wait_bytes(tiles.at[slot(x, zm(8)), 1], zr.at[8])
+    def zcopies(step):
+        for rel, dz, half in ZSENDS[step]:
+            src = tiles.at[slot(x, zm(rel))]
+            if half is not None:
+                src = src.at[half]
+            tsend_to(src, zsem.at[(rel - dz) % NZ if half != 1 else 0], dev(x, zm(dz), c, y))
+
+    def zwait(group):
+        for rel in ZGROUPS[group]:
+            src = tiles.at[slot(x, zm(rel))]
+            if rel == 8:
+                wait_bytes(src.at[0], zsem.at[8])
+                wait_bytes(src.at[1], zsem.at[0])
+            else:
+                wait_bytes(src, zsem.at[rel % NZ])
 
     def members(n):
-        if n == 0:
-            return [z]
-        if n == 8:
-            return [zm(8)]
-        return [zm(-n), zm(n)]
+        return [zm(rel) for rel in ZGROUPS[n]]
 
     partner = dev(x, z, oth, y)
 
@@ -232,16 +233,21 @@
             tsend_to(src, xl.at[zz], dev(xr_, z, c, y))
             tsend_to(src, xr.at[zz], dev(xl_, z, c, y))
             tsend_to(src, psem, partner)
+            if n == 4:
+                tsend_to(src.at[0], x2sem.at[0], dev(x2_, z, c, y))
+                tsend_to(src.at[1], x2sem.at[1], dev(x2_, z, c, y))
 
     def relay(n):
         for zz in members(n):
             src = tiles.at[slot(xl_, zz)]
             wait_bytes(src, xl.at[zz])
-            tsend_to(src.at[0], x2sem.at[0], dev(xr_, z, c, y))
+            if n < 4:
+                tsend_to(src.at[0], x2sem.at[0], dev(xr_, z, c, y))
             tsend_to(src, psem, partner)
             src = tiles.at[slot(xr_, zz)]
             wait_bytes(src, xr.at[zz])
-            tsend_to(src.at[1], x2sem.at[1], dev(xl_, z, c, y))
+            if n < 4:
+                tsend_to(src.at[1], x2sem.at[1], dev(xl_, z, c, y))
             tsend_to(src, psem, partner)
 
     src_id = x * NC + c
@@ -250,36 +256,43 @@
         zz = zm(d)
         for dx in range(NX):
             g = (x + dx) % NX
-            cp = rcopy(stage.at[:, zz * 4 + g], c2.at[src_id, z], a2s, a2r, dev(g, zz, OC, y))
+            cp = rcopy(stage.at[zz * 4 + g], c2.at[src_id, z], a2s, a2r, dev(g, zz, OC, y))
             if d or dx:
                 cp.start()
             else:
 
                 @pl.when(c == OC)
                 def _():
-                    pltpu.make_async_copy(stage.at[:, zz * 4 + g], c2.at[src_id, z], a2r).start()
+                    pltpu.make_async_copy(stage.at[zz * 4 + g], c2.at[src_id, z], a2r).start()
 
                 @pl.when(c != OC)
                 def _():
                     cp.start()
 
-    pl.semaphore_wait(rowsem, NX * NC - 1)
     wsend_first()
-    for s in range(1, 9):
-        ring_send(s)
-        for d in SENDS[s - 1]:
+    for n in range(4):
+        if n:
+            zwait(n)
+        zcopies(n)
+        forward(n)
+        if n == 0:
+            pl.semaphore_wait(rowsem, NX * NC - 1)
+        for d in SENDS[n]:
             col_send(d)
-        forward(s - 1)
-        if s >= 2:
-            relay(s - 2)
-        if s == 2:
+        if n >= 1:
+            relay(n - 1)
+        if n == 1:
             attended_send(0, quarter(orow), 0, 0)
-        if s == 6:
+        if n == 2:
             wrelay()
-        ring_wait(s)
-    forward(8)
-
-    relay(7)
+    zwait(4)
+    forward(4)
+    relay(3)
+    relay(4)
+    far2 = tiles.at[pl.ds(slot(x2_, 0), NZ)]
+    wait_bytes(far2.at[:, 0], x2sem.at[0])
+    wait_bytes(far2.at[:, 1], x2sem.at[1])
+    tsend_to(far2, psem, partner)
 
     @pl.when(c == OC)
     def _():
@@ -303,24 +316,25 @@
             p = jnp.exp2((s - m) * EXPC)
             l = jnp.sum(p, axis=1, keepdims=True)
             cfo[cols, :] = dot(p.astype(BF), vc) / l
-        obuf[...] = cfo[...].astype(BF).reshape(NX, NC, NZ, 8, HD)
-        lanes = pl.ds(pl.multiple_of(y * 2 * HD, HD), HD)
+        back = cfo[...].astype(BF).reshape(NX, NC, NZ, 8, HD)
+        for cc in range(NC):
+            obuf[:, :, cc] = back[:, cc]
+        lanes = pl.ds(pl.multiple_of(y * HD, HD), HD)
 
         def give_back(i, carry):
-            for dx in range(NX):
-                xx, zz = (x + dx) % NX, (z + i) % NZ
-                rcopy(
-                    obuf.at[xx, :, zz], abuf.at[:, (z % 4) * 4 + x, :, lanes], r1s, asem, dev(xx, zz, 1, z // 4)
-                ).start()
+            for zz in ((z + 8 - i) % NZ, (z + NZ - 7 + i) % NZ):
+                for dx in range(NX):
+                    xx = (x + dx) % NX
+                    rcopy(
+                        obuf.at[xx, zz],
+                        abuf.at[1, :, (z % 4) * 4 + x, :, lanes],
+                        r1s,
+                        asem.at[1],
+                        dev(xx, zz, 1, z // 4),
+                    ).start()
             return carry
 
-        lax.fori_loop(0, NZ, give_back, 0)
-
-    relay(8)
-    far2 = tiles.at[pl.ds(slot(x2_, 0), NZ)]
-    wait_bytes(far2.at[:, 0], x2sem.at[0])
-    wait_bytes(far2.at[:, 1], x2sem.at[1])
-    tsend_to(far2, psem, partner)
+        lax.fori_loop(0, NZ // 2, give_back, 0)
 
     wait_bytes(tiles.at[pl.ds(oth * 64, 64)], psem)
     for f in range(2):
@@ -340,26 +354,33 @@
             l = l_s[f, rs, :][:, :1] * shrink + jnp.sum(p, axis=1, keepdims=True)
             acc = acc_s[f, rs, :] * shrink + dot(p.astype(BF), farv[...])
             ofix[f, i * (QC // 8) : (i + 1) * (QC // 8)] = (acc / l).astype(BF).reshape(QC // 8, 8, HD)
-        attended_send(1 + f, quarter(ofix.at[f]), f, 1)
-
-
-    wait_bytes(wrows(yl, 1), wrsem.at[1])
+        attended_send(1 + f, quarter(ofix.at[f]), f, 1 - f)
+
+
     wait_bytes(wrows(yr, 0), wrsem.at[2])
     wait_bytes(wrows(y2, 0), wrsem.at[4])
+    wait_bytes(abuf.at[0], asem.at[0])
+    for i, at in enumerate((oth, c)):
+        a = abuf[0, at].reshape(128, 512)
+        for n in range(4):
+            part[i, :, n * 512 : (n + 1) * 512] = dot(a, wbuf[:512, n * 512 : (n + 1) * 512])
+    wait_bytes(wrows(yl, 1), wrsem.at[1])
     wait_bytes(wrows(y2, 1), wrsem.at[5])
-    wait_bytes(abuf, asem)
+    wait_bytes(abuf.at[1], asem.at[1])
     psends = []
-    ap = abuf[oth].reshape(128, 1024)
+    ap = abuf[1, oth].reshape(128, 512)
     for n in range(4):
-        pbuf[n] = dot(ap, wbuf[:, n * 512 : (n + 1) * 512]).astype(BF)
+        cols = slice(n * 512, (n + 1) * 512)
+        pbuf[n] = (part[0, :, cols] + dot(ap, wbuf[512:, cols])).astype(BF)
         cp = rcopy(pbuf.at[n], prcv.at[n], fsend.at[n], frecv.at[n], partner)
         cp.start()
         psends.append(cp)
-    ao = abuf[c].reshape(128, 1024)
+    ao = abuf[1, c].reshape(128, 512)
     for n in range(4):
-        po = dot(ao, wbuf[:, n * 512 : (n + 1) * 512])
+        cols = slice(n * 512, (n + 1) * 512)
+        po = part[1, :, cols] + dot(ao, wbuf[512:, cols])
         psends[n].wait_recv()
-        out[:, n * 512 : (n + 1) * 512] = (po + prcv[n].astype(F32)).astype(BF)
+        out[:, cols] = (po + prcv[n].astype(F32)).astype(BF)
 
     for cp in psends:
         cp.wait_send()
@@ -380,7 +401,7 @@
 
     @pl.when(c == OC)
     def _():
-        wait_bytes(stage.at[:, pl.ds(0, 63)], a2s)
+        wait_bytes(stage.at[pl.ds(0, 63)], a2s)
         wait_bytes(obuf, r1s)
 
 
@@ -404,10 +425,11 @@
             pltpu.VMEM((BLK, 512), BF),
             pltpu.VMEM((128, 2, 2, SUM, HD), BF),
             pltpu.VMEM((1024, 2048), BF),
-            pltpu.VMEM((2, 16, 8, 1024), BF),
-            pltpu.VMEM((3, 64, 8, HD), BF),
+            pltpu.VMEM((2, 2, 16, 8, 512), BF),
+            pltpu.VMEM((2, 128, 2048), F32),
+            pltpu.VMEM((64, 3, 8, HD), BF),
             pltpu.VMEM((NX * NC, NZ, 3, 8, HD), BF),
-            pltpu.VMEM((NX, NC, NZ, 8, HD), BF),
+            pltpu.VMEM((NX, NZ, NC, 8, HD), BF),
             pltpu.VMEM((64, 8, HD), BF),
             pltpu.VMEM((2, 64, 8, HD), BF),
             pltpu.VMEM((3, NBLK8, HD), F32),
@@ -419,8 +441,8 @@
             pltpu.VMEM((BLK, HD), BF),
             pltpu.VMEM((4, 128, 512), BF),
             pltpu.VMEM((4, 128, 512), BF),
-            dma((3,)), dma((9,)), dma((2,)), dma((6,)), dma((6,)), dma, dma((9,)), dma((9,)), dma((16,)), dma((16,)), dma((2,)), dma,
-            pltpu.SemaphoreType.REGULAR, dma, dma, dma, dma((3, 4)), dma, dma((4,)), dma((4,)),
+            dma((3,)), dma((9,)), dma((2,)), dma((6,)), dma((6,)), dma, dma((16,)), dma((16,)), dma((16,)), dma((2,)), dma,
+            pltpu.SemaphoreType.REGULAR, dma, dma, dma, dma((3, 4)), dma((2,)), dma((4,)), dma((4,)),
         ],
         compiler_params=pltpu.CompilerParams(
             collective_id=0, has_side_effects=True, vmem_limit_bytes=67043328

time: 75.1 us -> 67.7 us (0.901)
  the two profiles are of different devices: /device:TPU:1 before, /device:TPU:9 now
where the time goes in v3:
time: 67.7 us; the launch traced here: 67.5 us
  Pallas kernels  65.7 us (97%)
  local copies, waits for them, and re-layouts  1.88 us (3%)
    pallas_call x1, Pallas kernels, per_device(): pl.pallas_call(kernel, out_shape=jax.ShapeDtypeStruct((128, 2048), BF), i...  65.7 us
    unnamed x1, local copies, waits for them, and re-layouts  1.88 us

profile of v3, /device:TPU:9, one launch (start us, length us, event | category | flops | bytes accessed | tf_op | source)
XLA Modules:
  0.0 67.5 jit_solution(17331382217972487074)
XLA Ops:
  0.0 65.7 %shard_map.55 = bf16[128,2048]{1,0:T(8,128)(2,1)} custom-call(s32[1,2,16]{2,1,0:T(2,128)} %lists_h.1, bf16[512,512]{1,0:T(8,128)(2,1)} %q_h.1, bf16[512,512]{1,0:T(8,128)(2,1)} %k_h.1, bf16[512,512]{1,0:T(8,128)(2,1)} %v_h.1, bf16[64,8,512]{2,1,0:T(8,128)(2,1)} %bitcast.3, bf16[64,8,512]{2,1,0:T(8,128)(2,1)} %bitcast.4, bf16[64,8,512]{2,1,0:T(8,128)(2,1)} %bitcast.5, ...), custom_call_target="tpu_custom_call" | custom-call | tf_op jit(solution)/shard_map/pallas_call | solution.py:416
  65.7 1.9 %copy.7 = bf16[128,2048]{1,0:T(8,128)(2,1)} copy(bf16[128,2048]{1,0:T(8,128)(2,1)} %shard_map.55) | data formatting | bytes 1048576

commit v4 on v3

--- a/solution.py
+++ b/solution.py
@@ -25,7 +25,7 @@
     ((-6, 1, None), (6, -1, None), (-4, -1, None), (4, 1, None)),
     ((-7, 1, 0), (7, -1, 1)),
 )
-SENDS = ((8, 0, 1, -1), (7, -7, 6, -6), (5, -5, 4, -4), (3, -3, 2, -2))
+SENDS = ((8,7,-7,0),(6,-6,5,-5,4,-4),(3,-3,2,-2,1,-1),())
 BF = jnp.bfloat16
 F32 = jnp.float32
 
@@ -287,12 +287,6 @@
             wrelay()
     zwait(4)
     forward(4)
-    relay(3)
-    relay(4)
-    far2 = tiles.at[pl.ds(slot(x2_, 0), NZ)]
-    wait_bytes(far2.at[:, 0], x2sem.at[0])
-    wait_bytes(far2.at[:, 1], x2sem.at[1])
-    tsend_to(far2, psem, partner)
 
     @pl.when(c == OC)
     def _():
@@ -335,6 +329,13 @@
             return carry
 
         lax.fori_loop(0, NZ // 2, give_back, 0)
+
+    relay(3)
+    relay(4)
+    far2 = tiles.at[pl.ds(slot(x2_, 0), NZ)]
+    wait_bytes(far2.at[:, 0], x2sem.at[0])
+    wait_bytes(far2.at[:, 1], x2sem.at[1])
+    tsend_to(far2, psem, partner)
 
     wait_bytes(tiles.at[pl.ds(oth * 64, 64)], psem)
     for f in range(2):
@@ -405,6 +406,10 @@
         wait_bytes(obuf, r1s)
 
 
+def hand_over(a, b):
+    b[...] = a[...]
+
+
 NBLK8 = NX * NZ * NC * 8
 
 
@@ -413,7 +418,7 @@
     vm = pl.BlockSpec(memory_space=pltpu.VMEM)
     anys = pl.BlockSpec(memory_space=pl.ANY)
     dma = pltpu.SemaphoreType.DMA
-    return pl.pallas_call(
+    mixed = pl.pallas_call(
         kernel,
         out_shape=jax.ShapeDtypeStruct((128, 2048), BF),
         in_specs=[anys] * 8,
@@ -448,6 +453,15 @@
             collective_id=0, has_side_effects=True, vmem_limit_bytes=67043328
         ),
     )(summary_lists, queries, keys, values, q3, k3, v3, out_weight)
+    rows = pl.BlockSpec((64, 2048), lambda i: (i, 0))
+    return pl.pallas_call(
+        hand_over,
+        grid=(2,),
+        out_shape=jax.ShapeDtypeStruct((128, 2048), BF),
+        in_specs=[rows],
+        out_specs=rows,
+        compiler_params=pltpu.CompilerParams(vmem_limit_bytes=67043328),
+    )(mixed)
 
 
 def solution(mesh):

time: 67.7 us -> 67.2 us (level)
  the two profiles are of different devices: /device:TPU:9 before, /device:TPU:1 now
where the time goes in v4:
time: 67.2 us; the launch traced here: 67.1 us
  Pallas kernels  67 us (100%)
    pallas_call x1, Pallas kernels, per_device(): pl.pallas_call(kernel, out_shape=jax.ShapeDtypeStruct((128, 2048), BF), i...  65.3 us
    pallas_call x1, Pallas kernels, per_device(): pl.pallas_call(hand_over, grid=(2,), out_shape=jax.ShapeDtypeStruct((128,...  1.77 us

profile of v4, /device:TPU:1, one launch (start us, length us, event | category | flops | bytes accessed | tf_op | source)
XLA Modules:
  0.0 67.1 jit_solution(8929587304098814506)
XLA Ops:
  0.0 65.3 %shard_map.55.a = bf16[128,2048]{1,0:T(8,128)(2,1)} custom-call(s32[1,2,16]{2,1,0:T(2,128)} %lists_h.1, bf16[512,512]{1,0:T(8,128)(2,1)} %q_h.1, bf16[512,512]{1,0:T(8,128)(2,1)} %k_h.1, bf16[512,512]{1,0:T(8,128)(2,1)} %v_h.1, bf16[64,8,512]{2,1,0:T(8,128)(2,1)} %bitcast.3, bf16[64,8,512]{2,1,0:T(8,128)(2,1)} %bitcast.4, bf16[64,8,512]{2,1,0:T(8,128)(2,1)} %bitcast.5, ...), custom_call_target="tpu_custom_call" | custom-call | tf_op jit(solution)/shard_map/pallas_call | solution.py:421
  65.3 1.8 %shard_map.56 = bf16[128,2048]{1,0:T(8,128)(2,1)} custom-call(bf16[128,2048]{1,0:T(8,128)(2,1)} %shard_map.55.a), custom_call_target="tpu_custom_call" | custom-call | tf_op jit(solution)/shard_map/pallas_call | solution.py:457

commit v5 on v4

--- a/solution.py
+++ b/solution.py
@@ -25,7 +25,7 @@
     ((-6, 1, None), (6, -1, None), (-4, -1, None), (4, 1, None)),
     ((-7, 1, 0), (7, -1, 1)),
 )
-SENDS = ((8,7,-7,0),(6,-6,5,-5,4,-4),(3,-3,2,-2,1,-1),())
+SENDS = ((8, 7, -7, 0, 1, -1), (6, -6, 5, -5, 4, -4), (3, -3, 2, -2), ())
 BF = jnp.bfloat16
 F32 = jnp.float32
 

time: 67.2 us -> 67.2 us (level)
  no operation moved by 1% of the time
where the time goes in v5:
time: 67.2 us; the launch traced here: 67 us
  Pallas kernels  67 us (100%)
    pallas_call x1, Pallas kernels, per_device(): pl.pallas_call(kernel, out_shape=jax.ShapeDtypeStruct((128, 2048), BF), i...  65.2 us
    pallas_call x1, Pallas kernels, per_device(): pl.pallas_call(hand_over, grid=(2,), out_shape=jax.ShapeDtypeStruct((128,...  1.77 us

profile of v5, /device:TPU:1, one launch (start us, length us, event | category | flops | bytes accessed | tf_op | source)
XLA Modules:
  0.0 67.0 jit_solution(468867161404594684)
XLA Ops:
  0.0 65.2 %shard_map.55.a = bf16[128,2048]{1,0:T(8,128)(2,1)} custom-call(s32[1,2,16]{2,1,0:T(2,128)} %lists_h.1, bf16[512,512]{1,0:T(8,128)(2,1)} %q_h.1, bf16[512,512]{1,0:T(8,128)(2,1)} %k_h.1, bf16[512,512]{1,0:T(8,128)(2,1)} %v_h.1, bf16[64,8,512]{2,1,0:T(8,128)(2,1)} %bitcast.3, bf16[64,8,512]{2,1,0:T(8,128)(2,1)} %bitcast.4, bf16[64,8,512]{2,1,0:T(8,128)(2,1)} %bitcast.5, ...), custom_call_target="tpu_custom_call" | custom-call | tf_op jit(solution)/shard_map/pallas_call | solution.py:421
  65.2 1.8 %shard_map.56 = bf16[128,2048]{1,0:T(8,128)(2,1)} custom-call(bf16[128,2048]{1,0:T(8,128)(2,1)} %shard_map.55.a), custom_call_target="tpu_custom_call" | custom-call | tf_op jit(solution)/shard_map/pallas_call | solution.py:457
